TPU v7x, 256 devices: a whole 4x4x8 slice. The times are simulated.
256 devices in a mesh: leaf: 16 (over z, core), row: 4 (over x), col: 4 (over y).
Axes of the slice: x: 4, y: 4, z: 8, core: 2. Of those that a mesh axis runs over, the one named last changes fastest.
Arguments:
- rhs_leaf: bfloat16 [16, 8, 64, 2048], P('leaf', None, None, 'col'), may hold values from -6 to 6
- dinv_leaf: bfloat16 [16, 8, 2048, 2048], P('leaf', None, 'row', 'col'), as said below
- panel_leaf: bfloat16 [16, 8, 1024, 2048], P('leaf', None, 'col', 'row'), may hold values from -0.0234375 to 0.0234375
- counts: int32 [16, 8], P('leaf'), may hold values from 256 to 2048, as said below
- row_index: int32 [16, 8, 1024], P('leaf'), may hold values from 0 to 4095, as said below
- rhs_root: bfloat16 [64, 4096], P(None, 'col'), may hold values from -6 to 6
- dinv_root: bfloat16 [4096, 4096], P(('leaf', 'row')), as said below
Outputs:
- y_leaf: bfloat16 [16, 8, 64, 2048], P('leaf', None, None, 'row')
- y_root: bfloat16 [64, 4096], P(None, ('leaf', 'row'))
Inputs may be any that keep to these rules, and one draw needn't show every extreme that they name: `counts`: each subtree supernode has at least 256 columns; at least one supernode of every draw has all 2048. `row_index`: within one supernode the 1024 entries are distinct and increasing. `dinv_leaf`: each [2048, 2048] block is lower triangular with a nonzero diagonal. `dinv_root`: lower triangular with a nonzero diagonal.
All inputs are finite; a program needn't handle non-finite values.
Results may differ from a plain program's by a relative error of at most 0.0053.
Values may be sent and summed in bfloat16 or wider, within the bound.
A program may use at most 64 MiB of HBM per device.

v0:
```python
import jax
import jax.numpy as jnp
from jax import lax
from jax.sharding import PartitionSpec as P


def copy_for_each(array, axis):
    copies = jnp.broadcast_to(array, (lax.axis_size(axis), *array.shape))
    return lax.all_to_all(copies, axis, split_axis=0, concat_axis=0, tiled=True)


def taken_together(array, axis):
    return copy_for_each(array, axis).sum(axis=0)


def cut_along(array, dim, size):
    before, after = (array.shape[:dim], array.shape[dim + 1 :])
    return jnp.moveaxis(array.reshape(*before, size, -1, *after), dim, 0)


def sum_at_owner(array, axis, dim):
    size = lax.axis_size(axis)
    tiles = lax.all_to_all(cut_along(array, dim, size), axis, 0, 0, tiled=True)
    return jnp.sum(tiles, axis=0)


def padded_to(lines, size):
    spare = -len(lines) % size
    return jnp.pad(lines, [(0, spare)] + [(0, 0)] * (lines.ndim - 1))


def in_order(tiles, dim):
    dims = list(tiles.shape[1:])
    dims[dim] *= tiles.shape[0]
    return jnp.moveaxis(tiles, 0, dim).reshape(dims)


def gathered_copies(array, axis, dim):
    return in_order(copy_for_each(array, axis), dim)


def total_of(array, axes):
    lines = array.reshape(-1, array.shape[-1])
    own = sum_at_owner(padded_to(lines, lax.axis_size(axes)), axes, 0)
    whole = gathered_copies(own, axes, 0)
    return whole[: len(lines)].reshape(array.shape)


def local(rhs_leaf, dinv_leaf, panel_leaf, counts, row_index, rhs_root, dinv_root):
    width_col = rhs_leaf.shape[3]
    width_row = dinv_leaf.shape[2]
    panel_rows = panel_leaf.shape[2]
    columns = rhs_root.shape[0]
    sep_width = rhs_root.shape[1] * lax.axis_size("col")
    limit = counts[0][:, None, None]
    col_slots = lax.axis_index("col") * width_col + lax.iota(jnp.int32, width_col)
    masked = jnp.where(col_slots[None, None, :] < limit, rhs_leaf[0], jnp.zeros((), jnp.bfloat16))
    partial_value = jnp.einsum(
        "kbj,kij->kbi", masked, dinv_leaf[0], preferred_element_type=jnp.float32
    )
    summed = taken_together(partial_value, "col")
    row_slots = lax.axis_index("row") * width_row + lax.iota(jnp.int32, width_row)
    live_rows = (row_slots[None, None, :] < limit).astype(jnp.float32)
    solved = (summed * live_rows).astype(jnp.bfloat16)
    update = jnp.einsum("kbi,kri->kbr", solved, panel_leaf[0], preferred_element_type=jnp.float32)
    offset = lax.axis_index("col") * panel_rows
    targets = lax.dynamic_slice_in_dim(row_index[0], offset, panel_rows, 1)
    flat_update = jnp.transpose(update, (1, 0, 2)).reshape(columns, -1)
    accum = jnp.zeros((columns, sep_width), jnp.float32).at[:, targets.reshape(-1)].add(flat_update)
    piece = sum_at_owner(accum, "col", 1)
    share = total_of(piece, ("leaf", "row"))
    reduced = (rhs_root.astype(jnp.float32) - share).astype(jnp.bfloat16)
    whole_reduced = gathered_copies(reduced, "col", 1)
    y_root = jnp.dot(whole_reduced, dinv_root.T, preferred_element_type=jnp.float32).astype(
        jnp.bfloat16
    )
    return (solved[None], y_root)


def solution(mesh):
    in_specs = (
        P("leaf", None, None, "col"),
        P("leaf", None, "row", "col"),
        P("leaf", None, "col", "row"),
        P("leaf", None),
        P("leaf", None, None),
        P(None, "col"),
        P(("leaf", "row"), None),
    )
    out_specs = (P("leaf", None, None, "row"), P(None, ("leaf", "row")))
    return jax.shard_map(local, mesh=mesh, in_specs=in_specs, out_specs=out_specs, check_vma=False)
```

profile of v0, /device:TPU:32, one launch (start us, length us, event | category | flops | bytes accessed | tf_op | source)
XLA Modules:
  0.0 168.4 jit_solution(12648357702584305741)
XLA Ops:
  0.6 0.0 copy-start
  0.7 0.9 compare_convert_fusion
  1.5 3.7 %fusion = f32[8,64,512]{2,1,0:T(8,128)S(1)} fusion(bf16[1,8,512,512]{3,2,1,0:T(8,128)(2,1)} %param.8, bf16[1,8,64,512]{3,2,1,0:T(8,128)(2,1)} %param.7, pred[8,512]{1,0:T(8,128)(4,1)S(1)} %get-tuple-element.3), kind=kOutput, calls=%fused_computation.1 | convolution fusion | flops 268697600 | bytes 5771264 | tf_op jit(solution)/shard_map/kbj,kij->kbi/dot_general | solution.py:58
  5.3 2.5 %broadcast_in_dim.30 = f32[4,8,64,512]{3,2,1,0:T(8,128)} broadcast(f32[8,64,512]{2,1,0:T(8,128)S(1)} %fusion), dimensions={1,2,3} | broadcast | bytes 5242880 | tf_op jit(solution)/shard_map/broadcast_in_dim | solution.py:8
  7.8 4.9 %all-to-all-start = ((f32[4,8,64,512]{3,2,1,0:T(8,128)}), f32[4,8,64,512]{3,2,1,0:T(8,128)}, u32[]{:S(2)}, u32[]{:S(2)}) async-start(f32[4,8,64,512]{3,2,1,0:T(8,128)} %broadcast_in_dim.30), calls=%async_computation | async-start | bytes 8388608 | tf_op jit(solution)/shard_map/all_to_all | solution.py:9
  12.6 0.7 dynamic-slice_bitcast_fusion
  13.4 48.4 %all-to-all-done = f32[4,8,64,512]{3,2,1,0:T(8,128)} async-done(((f32[4,8,64,512]{3,2,1,0:T(8,128)}), f32[4,8,64,512]{3,2,1,0:T(8,128)}, u32[]{:S(2)}, u32[]{:S(2)}) %all-to-all-start) | async-done | bytes 4194336 | tf_op jit(solution)/shard_map/all_to_all | solution.py:9
  61.8 2.8 %reduce_sum.29 = f32[8,64,512]{2,1,0:T(8,128)S(1)} reduce(f32[4,8,64,512]{3,2,1,0:T(8,128)} %all-to-all-done, f32[]{:T(128)} %constant.5.clone.1), dimensions={0}, to_apply=%region_0.1 | reduce | flops 786432 | bytes 5242884 | tf_op jit(solution)/shard_map/reduce_sum | solution.py:13
  64.6 0.0 copy-done
  64.6 0.7 fusion.4
  65.3 0.9 copy.25
  66.2 2.4 %copy.18 = f32[2048,64]{1,0:T(8,128)} copy(f32[2048,64]{0,1:T(8,128)} %bitcast.41) | data formatting | bytes 1048576 | tf_op jit(solution)/shard_map/reshape | solution.py:68
  68.5 13.3 %scatter_custom_fusion = f32[64,4096]{0,1:T(8,128)} fusion(s32[2048]{0:T(1024)S(1)} %bitcast.45, f32[2048,64]{1,0:T(8,128)} %copy.18, f32[]{:T(128)} %constant.5.clone.1), kind=kCustom, calls=%fused_computation.10 | custom fusion | flops 131072 | bytes 1049088 | tf_op jit(solution)/shard_map/scatter-add | solution.py:69
  81.8 3.2 %copy.19 = f32[64,4,1024]{2,0,1:T(8,128)} copy(f32[64,4,1024]{0,2,1:T(8,128)} %bitcast.39) | data formatting | bytes 2097152 | tf_op jit(solution)/shard_map/reshape | solution.py:18
  85.0 18.8 %all_to_all.25 = f32[4,64,1024]{2,1,0:T(8,128)} all-to-all(f32[4,64,1024]{2,1,0:T(8,128)} %bitcast.40), channel_id=1, replica_groups=mesh['leaf'=16,'row'=4,'col'=4] {'col'}, dimensions={0} | all-to-all | bytes 2097152 | tf_op jit(solution)/shard_map/all_to_all | solution.py:23
  103.8 0.0 copy-start.1
  103.8 1.3 reduce_sum.31
  105.1 1.0 copy.24
  106.1 1.2 copy.21
  107.4 24.7 %all_to_all.26 = f32[64,1,1024]{2,1,0:T(1,128)} all-to-all(f32[64,1,1024]{2,1,0:T(1,128)S(1)} %copy.21), channel_id=1, replica_groups=mesh['leaf'=16,'row'=4,'col'=4] {'leaf','row'}, dimensions={0} | all-to-all | bytes 524288 | tf_op jit(solution)/shard_map/all_to_all | solution.py:23
  132.1 1.1 reduce_sum.32
  133.2 0.1 broadcast_in_dim.32
  133.3 17.6 %all_to_all.27 = f32[64,1,1024]{2,1,0:T(1,128)S(1)} all-to-all(f32[64,1,1024]{2,1,0:T(1,128)S(1)} %broadcast_in_dim.32), channel_id=1, replica_groups=mesh['leaf'=16,'row'=4,'col'=4] {'leaf','row'}, dimensions={0} | all-to-all | bytes 524288 | tf_op jit(solution)/shard_map/all_to_all | solution.py:9
  151.0 0.0 copy-done.1
  151.0 0.1 fusion.12
  151.0 0.9 broadcast_in_dim.33
  151.9 4.1 %all-to-all-start.4 = ((bf16[4,64,1024]{2,1,0:T(8,128)(2,1)}), bf16[4,64,1024]{2,1,0:T(8,128)(2,1)}, u32[]{:S(2)}, u32[]{:S(2)}) async-start(bf16[4,64,1024]{2,1,0:T(8,128)(2,1)} %broadcast_in_dim.33), calls=%async_computation.4 | async-start | bytes 1048576 | tf_op jit(solution)/shard_map/all_to_all | solution.py:9
  156.0 0.9 fusion.7
  157.0 8.4 %all-to-all-done.4 = bf16[4,64,1024]{2,1,0:T(8,128)(2,1)} async-done(((bf16[4,64,1024]{2,1,0:T(8,128)(2,1)}), bf16[4,64,1024]{2,1,0:T(8,128)(2,1)}, u32[]{:S(2)}, u32[]{:S(2)}) %all-to-all-start.4) | async-done | bytes 524320 | tf_op jit(solution)/shard_map/all_to_all | solution.py:9
  165.3 1.1 copy.26
  166.4 2.0 %convolution_convert_fusion = bf16[64,64]{1,0:T(8,128)(2,1)} fusion(bf16[64,4096]{1,0:T(8,128)(2,1)S(1)} %bitcast.43, bf16[64,4096]{1,0:T(8,128)(2,1)} %param.13), kind=kOutput, calls=%fused_computation.6 | convolution fusion | flops 33558528 | bytes 1056768 | tf_op jit(solution)/shard_map/dot_general | solution.py:74
  (3 shorter events, 0.0 us)
Async XLA Ops:
  0.6 63.9 %copy-start = (bf16[1,8,256,512]{3,2,1,0:T(8,128)(2,1)S(1)}, bf16[1,8,256,512]{3,2,1,0:T(8,128)(2,1)}, u32[]{:S(2)}) copy-start(bf16[1,8,256,512]{3,2,1,0:T(8,128)(2,1)} %param.9) | copy-start | bytes 6291460
  7.8 54.0 %all-to-all-start = ((f32[4,8,64,512]{3,2,1,0:T(8,128)}), f32[4,8,64,512]{3,2,1,0:T(8,128)}, u32[]{:S(2)}, u32[]{:S(2)}) async-start(f32[4,8,64,512]{3,2,1,0:T(8,128)} %broadcast_in_dim.30), calls=%async_computation | async-start | bytes 8388608 | tf_op jit(solution)/shard_map/all_to_all | solution.py:9
  103.8 47.2 %copy-start.1 = (bf16[64,1024]{1,0:T(8,128)(2,1)S(1)}, bf16[64,1024]{1,0:T(8,128)(2,1)}, u32[]{:S(2)}) copy-start(bf16[64,1024]{1,0:T(8,128)(2,1)} %param.12) | copy-start | bytes 393220
  151.9 13.4 %all-to-all-start.4 = ((bf16[4,64,1024]{2,1,0:T(8,128)(2,1)}), bf16[4,64,1024]{2,1,0:T(8,128)(2,1)}, u32[]{:S(2)}, u32[]{:S(2)}) async-start(bf16[4,64,1024]{2,1,0:T(8,128)(2,1)} %broadcast_in_dim.33), calls=%async_computation.4 | async-start | bytes 1048576 | tf_op jit(solution)/shard_map/all_to_all | solution.py:9
where the time goes:
time: 169 us; the launch traced here: 168 us
  blocking collectives  61.1 us (36%)
  waiting for transfers between devices  56.8 us (34%)
  other arithmetic  20.4 us (12%)
  local copies, waits for them, and re-layouts  13.9 us (8%)
  starting transfers between devices  8.98 us (5%)
  matrix products  6.45 us (4%)
    all_to_all x2, waiting for transfers between devices, copy_for_each(): return lax.all_to_all(copies, axis, split_axis=0, concat_axis=0, tiled=True)  56.8 us
    all_to_all x2, blocking collectives, sum_at_owner(): tiles = lax.all_to_all(cut_along(array, dim, size), axis, 0, 0, tiled=True)  43.5 us
    all_to_all x1, blocking collectives, copy_for_each(): return lax.all_to_all(copies, axis, split_axis=0, concat_axis=0, tiled=True)  17.6 us
    scatter-add x1, other arithmetic, local(): jnp.zeros((columns, sep_width), jnp.float32).at[:, targets.reshape(-1)]  13.3 us
    all_to_all x2, starting transfers between devices, copy_for_each(): return lax.all_to_all(copies, axis, split_axis=0, concat_axis=0, tiled=True)  8.98 us
    reshape x2, local copies, waits for them, and re-layouts, cut_along(): return jnp.moveaxis(array.reshape(*before, size, -1, *after), dim, 0)  4.4 us
    dot_general x1, matrix products, local(): jnp.einsum('kbj,kij->kbi', masked, dinv_leaf[0], preferred_element_type=j...  3.72 us
    broadcast_in_dim x3, local copies, waits for them, and re-layouts, copy_for_each(): copies = jnp.broadcast_to(array, (lax.axis_size(axis), *array.shape))  3.52 us
  transfers between devices with their start and end apart: 2, of which 2 were waited for; matrix products, arithmetic and copies ran while one was open for 1% of the time, Pallas kernels for 0%

commit v1 on v0

v1 whole, which is shorter than its diff:
```python
import jax
import jax.numpy as jnp
from jax import lax
from jax.experimental import pallas as pl
from jax.experimental.pallas import tpu as pltpu
from jax.sharding import PartitionSpec as P

BF16 = jnp.bfloat16
F32 = jnp.float32
MESH = pl.DeviceIdType.MESH
NODES, B, WC, PR, ROOT = 8, 64, 512, 256, 4096
TILE = 512


def dot_nt(a, b):
    return lax.dot_general(a, b, (((1,), (1,)), ((), ())), preferred_element_type=F32)


def body(counts, rhs_h, dinv_h, panel_h, rows_h, rroot_h, droot_h, yleaf_h, yroot_o,
         rhs, dinv, panel, rows, rroot, droot, s1, r1, s2, r2, y, hot, upd, acc,
         cs, cr, zs, zr, red, part, in_sem, s1_s, s1_r, s2_s, s2_r, y_sem,
         c_s, c_r, z_s, z_r, g_s, g_r, p_s, p_r):
    leaf, r, c = lax.axis_index("leaf"), lax.axis_index("row"), lax.axis_index("col")
    z, k = leaf // 2, leaf % 2
    near = c + 1 - 2 * (c % 2)
    far = 3 - c

    def load(src, dst, i):
        copy = pltpu.make_async_copy(src, dst, in_sem.at[i])
        copy.start()
        return copy

    order = [s for i in range(NODES // 2) for s in (i, i + NODES // 2)]
    loads = {}
    loads["rhs"] = load(rhs_h.at[0], rhs, 0)
    for s in order:
        loads["d", s] = load(dinv_h.at[0, s], dinv.at[s], 1 + s)
    cut = pl.multiple_of(c * PR, PR)
    loads["rows"] = load(rows_h.at[0, :, pl.ds(cut, PR)], rows, 17)
    for s in order:
        loads["p", s] = load(panel_h.at[0, s], panel.at[s], 9 + s)
    loads["rroot"] = load(rroot_h, rroot, 18)
    cut = pl.multiple_of(c * 1024, 1024)
    loads["droot"] = load(droot_h.at[:, pl.ds(cut, 1024)], droot, 19)

    def plane(dk, dr, dc):
        return (z * 2 + (k + dk) % 2, (r + dr) % 4, (c + dc) % 4)

    shifts = [(dk, dr, dc) for dc in (2, 1, 3, 0) for dr in (2, 1, 3, 0) for dk in (1, 0)]
    barrier = pltpu.get_barrier_semaphore()
    for shift in shifts[:-1]:
        pl.semaphore_signal(barrier, inc=1, device_id=plane(*shift), device_id_type=MESH)
    for dz in range(1, 8):
        pl.semaphore_signal(barrier, inc=1, device_id=(((z + dz) % 8) * 2 + k, r, c), device_id_type=MESH)
    pl.semaphore_wait(barrier, 38)

    def remote(src, dst, ss, rs, where):
        copy = pltpu.make_async_remote_copy(
            src_ref=src, dst_ref=dst, send_sem=ss, recv_sem=rs, device_id=where, device_id_type=MESH)
        copy.start()
        return copy

    lane = lax.broadcasted_iota(jnp.int32, (B, WC), 1)
    sends = []
    first, second = {}, {}
    loads["rhs"].wait()
    for s in order:
        loads["d", s].wait()
        masked = jnp.where(lane + c * WC < counts[0, s], rhs[s].astype(F32), 0.0).astype(BF16)
        s1[s] = dot_nt(masked, dinv[s]).astype(BF16)
        to = near if s < NODES // 2 else far
        first[s] = remote(s1.at[s], r1.at[s], s1_s.at[s], s1_r.at[s], (leaf, r, to))
    loads["rows"].wait()
    for i in range(NODES // 2):
        low = rows[i:i + 1, :]
        high = rows[i + NODES // 2:i + NODES // 2 + 1, :]

        def make(t, _, i=i, low=low, high=high):
            at = lax.broadcasted_iota(jnp.int32, (TILE, PR), 0) + t * TILE
            span = pl.ds(pl.multiple_of(t * TILE, TILE), TILE)
            hot[i, span, 0:PR] = jnp.where(at == low, 1.0, 0.0).astype(BF16)
            hot[i, span, PR:2 * PR] = jnp.where(at == high, 1.0, 0.0).astype(BF16)
            return 0

        lax.fori_loop(0, ROOT // TILE, make, 0)
        for s in (i, i + NODES // 2):
            first[s].wait_recv()
            s2[s] = (s1[s].astype(F32) + r1[s].astype(F32)).astype(BF16)
            to = far if s < NODES // 2 else near
            second[s] = remote(s2.at[s], r2.at[s], s2_s.at[s], s2_r.at[s], (leaf, r, to))
    outs = []
    for i in range(NODES // 2):
        for h, s in enumerate((i, i + NODES // 2)):
            second[s].wait_recv()
            total = s2[s].astype(F32) + r2[s].astype(F32)
            solved = jnp.where(lane + r * WC < counts[0, s], total, 0.0).astype(BF16)
            y[s] = solved
            out = pltpu.make_async_copy(y.at[s], yleaf_h.at[0, s], y_sem.at[s])
            out.start()
            outs.append(out)
            loads["p", s].wait()
            upd[:, h * PR:(h + 1) * PR] = dot_nt(solved, panel[s]).astype(BF16)
        if i < NODES // 2 - 1:

            def add(t, _, i=i):
                span = pl.ds(pl.multiple_of(t * TILE, TILE), TILE)
                got = dot_nt(upd[...], hot[i, span, :])
                acc[t] = got if i == 0 else acc[t] + got
                return 0

            lax.fori_loop(0, ROOT // TILE, add, 0)
        else:
            pieces = {}
            for dc in (2, 1, 3, 0):
                cb = (c + dc) % 4
                for half in range(2):
                    t = cb * 2 + half
                    span = pl.ds(pl.multiple_of(t * TILE, TILE), TILE)
                    tile = (acc[t] + dot_nt(upd[...], hot[i, span, :])).astype(BF16)
                    for q in range(4):
                        cs[cb * 8 + half * 4 + q] = tile[:, q * 128:(q + 1) * 128]
                for dr in (2, 1, 3, 0):
                    for dk in (1, 0):
                        if dc == 0 and dr == 0 and dk == 0:
                            continue
                        kb, rb = (k + dk) % 2, (r + dr) % 4
                        j = dc * 8 + dr * 2 + dk
                        pieces[j] = remote(cs.at[cb * 8 + rb * 2 + kb], cr.at[j], c_s.at[j], c_r.at[j],
                                           (z * 2 + kb, rb, cb))
    mine = r * 2 + k
    total = cs[c * 8 + mine].astype(F32)
    for j in pieces:
        pieces[j].wait_recv()
        total = total + cr[j].astype(F32)
    zs[...] = total.astype(BF16)
    zcopies = []
    for dz in (4, 3, 5, 2, 6, 1, 7):
        zcopies.append(remote(zs, zr.at[dz], z_s.at[dz], z_r.at[dz], (((z + dz) % 8) * 2 + k, r, c)))
    loads["rroot"].wait()
    total = rroot[:, pl.ds(pl.multiple_of(mine * 128, 128), 128)].astype(F32) - zs[...].astype(F32)
    for dz, copy in zip((4, 3, 5, 2, 6, 1, 7), zcopies):
        copy.wait_recv()
        total = total - zr[dz].astype(F32)
    red[mine] = total.astype(BF16)
    gathers = []
    for dr in (2, 1, 3, 0):
        for dk in (1, 0):
            if dr == 0 and dk == 0:
                continue
            j = dr * 2 + dk
            gathers.append(remote(red.at[mine], red.at[mine], g_s.at[j], g_r.at[j], plane(dk, dr, 0)))
    loads["droot"].wait()
    for copy in gathers:
        copy.wait_recv()
    whole = dot_nt(red[0], droot[:, 0:128])
    for q in range(1, 8):
        whole = whole + dot_nt(red[q], droot[:, q * 128:(q + 1) * 128])
    part[c] = whole
    shares = []
    for dc in (2, 1, 3):
        shares.append(remote(part.at[c], part.at[c], p_s.at[dc], p_r.at[dc], (leaf, r, (c + dc) % 4)))
    for copy in shares:
        copy.wait_recv()
    yroot_o[...] = (((part[0] + part[1]) + part[2]) + part[3]).astype(BF16)
    for copies in (first.values(), second.values(), pieces.values(), zcopies, gathers, shares):
        for copy in copies:
            copy.wait_send()
    for out in outs:
        out.wait()


def local(rhs_leaf, dinv_leaf, panel_leaf, counts, row_index, rhs_root, dinv_root):
    anywhere = pl.BlockSpec(memory_space=pl.ANY)
    dma = pltpu.SemaphoreType.DMA
    return pl.pallas_call(
        body,
        out_shape=(jax.ShapeDtypeStruct((1, NODES, B, WC), BF16), jax.ShapeDtypeStruct((B, 64), BF16)),
        in_specs=[pl.BlockSpec(memory_space=pltpu.SMEM)] + [anywhere] * 6,
        out_specs=(anywhere, pl.BlockSpec(memory_space=pltpu.VMEM)),
        scratch_shapes=[
            pltpu.VMEM((NODES, B, WC), BF16),
            pltpu.VMEM((NODES, WC, WC), BF16),
            pltpu.VMEM((NODES, PR, WC), BF16),
            pltpu.VMEM((NODES, PR), jnp.int32),
            pltpu.VMEM((B, 1024), BF16),
            pltpu.VMEM((64, 1024), BF16),
            pltpu.VMEM((NODES, B, WC), BF16),
            pltpu.VMEM((NODES, B, WC), BF16),
            pltpu.VMEM((NODES, B, WC), BF16),
            pltpu.VMEM((NODES, B, WC), BF16),
            pltpu.VMEM((NODES, B, WC), BF16),
            pltpu.VMEM((NODES // 2, ROOT, 2 * PR), BF16),
            pltpu.VMEM((B, 2 * PR), BF16),
            pltpu.VMEM((ROOT // TILE, B, TILE), F32),
            pltpu.VMEM((32, B, 128), BF16),
            pltpu.VMEM((32, B, 128), BF16),
            pltpu.VMEM((B, 128), BF16),
            pltpu.VMEM((8, B, 128), BF16),
            pltpu.VMEM((8, B, 128), BF16),
            pltpu.VMEM((4, B, 64), F32),
            dma((20,)), dma((8,)), dma((8,)), dma((8,)), dma((8,)), dma((8,)),
            dma((32,)), dma((32,)), dma((8,)), dma((8,)), dma((8,)), dma((8,)), dma((4,)), dma((4,)),
        ],
        compiler_params=pltpu.CompilerParams(
            collective_id=0, has_side_effects=True, vmem_limit_bytes=60 * 1024 * 1024),
        name="substitute",
    )(counts, rhs_leaf, dinv_leaf, panel_leaf, row_index, rhs_root, dinv_root)


def solution(mesh):
    in_specs = (
        P("leaf", None, None, "col"),
        P("leaf", None, "row", "col"),
        P("leaf", None, "col", "row"),
        P("leaf", None),
        P("leaf", None, None),
        P(None, "col"),
        P(("leaf", "row"), None),
    )
    out_specs = (P("leaf", None, None, "row"), P(None, ("leaf", "row")))
    return jax.shard_map(local, mesh=mesh, in_specs=in_specs, out_specs=out_specs, check_vma=False)
```

time: 169 us -> 57.2 us (0.34)
  blocking collectives: 61.1 us -> 0 us
  waiting for transfers between devices: 56.8 us -> 0 us
  Pallas kernels: 0 us -> 52.5 us
  other arithmetic: 20.4 us -> 0 us
  local copies, waits for them, and re-layouts: 13.9 us -> 3.19 us
  starting transfers between devices: 8.98 us -> 0 us
  matrix products: 6.45 us -> 0 us
    all_to_all x3 -> x0, blocking collectives: 61.1 us -> none  [the longest x2 43.5 us: sum_at_owner(): tiles = lax.all_to_all(cut_along(array, dim, size), axis, 0, 0, tiled=True)]
    all_to_all x2 -> x0, waiting for transfers between devices: 56.8 us -> none  [copy_for_each(): return lax.all_to_all(copies, axis, split_axis=0, concat_axis=0, tiled=True)]
    pallas_call x0 -> x1, Pallas kernels: none -> 52.5 us  [local(): pl.pallas_call(body, out_shape=(jax.ShapeDtypeStruct((1, NODES, B, WC), B...]
    scatter-add x1 -> x0, other arithmetic: 13.3 us -> none  [local(): jnp.zeros((columns, sep_width), jnp.float32).at[:, targets.reshape(-1)]]
    all_to_all x2 -> x0, starting transfers between devices: 8.98 us -> none  [copy_for_each(): return lax.all_to_all(copies, axis, split_axis=0, concat_axis=0, tiled=True)]
    reshape x5 -> x0, local copies, waits for them, and re-layouts: 8.7 us -> none  [the longest x2 4.4 us: cut_along(): return jnp.moveaxis(array.reshape(*before, size, -1, *after), dim, 0)]
    dot_general x3 -> x0, matrix products: 6.45 us -> none  [the longest x1 3.72 us: local(): jnp.einsum('kbj,kij->kbi', masked, dinv_leaf[0], preferred_element_type=j...]
    reduce_sum x3 -> x0, other arithmetic: 5.26 us -> none  [the longest x1 2.79 us: taken_together(): return copy_for_each(array, axis).sum(axis=0)]
  transfers between devices with their start and end apart: 2 -> 0, of which waited for: 2 -> 0; matrix products, arithmetic and copies ran while one was open for 1% -> 0% of each run, Pallas kernels for 0% -> 0%
where the time goes in v1:
time: 57.2 us; the launch traced here: 56.3 us
  Pallas kernels  52.5 us (92%)
  local copies, waits for them, and re-layouts  3.19 us (6%)
  between operations  0.64 us (1%)
    pallas_call x1, Pallas kernels, local(): pl.pallas_call(body, out_shape=(jax.ShapeDtypeStruct((1, NODES, B, WC), B...  52.5 us
    unnamed x2, local copies, waits for them, and re-layouts  3.19 us

profile of v1, /device:TPU:32, one launch (start us, length us, event | category | flops | bytes accessed | tf_op | source)
XLA Modules:
  0.0 56.3 jit_solution(8342041243292372558)
XLA Ops:
  0.6 52.5 %substitute.1 = (bf16[1,8,64,512]{3,2,1,0:T(8,128)(2,1)}, bf16[64,64]{1,0:T(8,128)(2,1)}) custom-call(s32[1,8]{1,0:T(1,128)} %counts.1, bf16[1,8,64,512]{3,2,1,0:T(8,128)(2,1)} %rhs_h.1, bf16[1,8,512,512]{3,2,1,0:T(8,128)(2,1)} %dinv_h.1, bf16[1,8,256,512]{3,2,1,0:T(8,128)(2,1)} %panel_h.1, s32[1,8,1024]{2,1,0:T(8,128)} %rows_h.1, bf16[64,1024]{1,0:T(8,128)(2,1)} %rroot_h.1, ...), custom_call_target="tpu_custom_call" | custom-call | tf_op jit(solution)/shard_map/substitute/pallas_call | solution.py:175
  53.1 1.9 %copy.11 = bf16[1,8,64,512]{3,2,1,0:T(8,128)(2,1)} copy(bf16[1,8,64,512]{3,2,1,0:T(8,128)(2,1)} %get-tuple-element.4) | data formatting | bytes 1048576
  55.0 1.3 %copy.12 = bf16[64,64]{1,0:T(8,128)(2,1)} copy(bf16[64,64]{1,0:T(8,128)(2,1)} %get-tuple-element.5) | data formatting | bytes 16384

commit v2 on v1

--- a/solution.py
+++ b/solution.py
@@ -12,6 +12,10 @@
 TILE = 512
 
 
+def dot_nn(a, b):
+    return lax.dot_general(a, b, (((1,), (0,)), ((), ())), preferred_element_type=F32)
+
+
 def dot_nt(a, b):
     return lax.dot_general(a, b, (((1,), (1,)), ((), ())), preferred_element_type=F32)
 
@@ -19,7 +23,7 @@
 def body(counts, rhs_h, dinv_h, panel_h, rows_h, rroot_h, droot_h, yleaf_h, yroot_o,
          rhs, dinv, panel, rows, rroot, droot, s1, r1, s2, r2, y, hot, upd, acc,
          cs, cr, zs, zr, red, part, in_sem, s1_s, s1_r, s2_s, s2_r, y_sem,
-         c_s, c_r, z_s, z_r, g_s, g_r, p_s, p_r):
+         c_s, c_r, z_s, z_r, g_s, g_r, p_s, p_r, relay):
     leaf, r, c = lax.axis_index("leaf"), lax.axis_index("row"), lax.axis_index("col")
     z, k = leaf // 2, leaf % 2
     near = c + 1 - 2 * (c % 2)
@@ -46,13 +50,20 @@
     def plane(dk, dr, dc):
         return (z * 2 + (k + dk) % 2, (r + dr) % 4, (c + dc) % 4)
 
-    shifts = [(dk, dr, dc) for dc in (2, 1, 3, 0) for dr in (2, 1, 3, 0) for dk in (1, 0)]
+    line_y = [plane(0, 0, dc) for dc in (1, 2, 3)]
+    line_x = [plane(0, dr, 0) for dr in (1, 2, 3)]
+    line_z = [(((z + dz) % 8) * 2 + k, r, c) for dz in (1, 7)]
+    pair = [plane(1, 0, 0)]
     barrier = pltpu.get_barrier_semaphore()
-    for shift in shifts[:-1]:
-        pl.semaphore_signal(barrier, inc=1, device_id=plane(*shift), device_id_type=MESH)
-    for dz in range(1, 8):
-        pl.semaphore_signal(barrier, inc=1, device_id=(((z + dz) % 8) * 2 + k, r, c), device_id_type=MESH)
-    pl.semaphore_wait(barrier, 38)
+    for where in line_y + line_x + pair + line_z:
+        pl.semaphore_signal(barrier, inc=1, device_id=where, device_id_type=MESH)
+
+    def tell(i, peers):
+        for where in peers:
+            pl.semaphore_signal(relay.at[i], inc=1, device_id=where, device_id_type=MESH)
+
+    def heard(i, count):
+        pl.semaphore_wait(relay.at[i], count)
 
     def remote(src, dst, ss, rs, where):
         copy = pltpu.make_async_remote_copy(
@@ -61,7 +72,6 @@
         return copy
 
     lane = lax.broadcasted_iota(jnp.int32, (B, WC), 1)
-    sends = []
     first, second = {}, {}
     loads["rhs"].wait()
     for s in order:
@@ -69,17 +79,21 @@
         masked = jnp.where(lane + c * WC < counts[0, s], rhs[s].astype(F32), 0.0).astype(BF16)
         s1[s] = dot_nt(masked, dinv[s]).astype(BF16)
         to = near if s < NODES // 2 else far
+        if s == order[0]:
+            pl.semaphore_wait(barrier, 9)
+            tell(0, line_x)
+            tell(2, line_z)
         first[s] = remote(s1.at[s], r1.at[s], s1_s.at[s], s1_r.at[s], (leaf, r, to))
     loads["rows"].wait()
+    targets = jnp.transpose(rows[...])
     for i in range(NODES // 2):
-        low = rows[i:i + 1, :]
-        high = rows[i + NODES // 2:i + NODES // 2 + 1, :]
+        low = targets[:, i:i + 1]
+        high = targets[:, i + NODES // 2:i + NODES // 2 + 1]
 
         def make(t, _, i=i, low=low, high=high):
-            at = lax.broadcasted_iota(jnp.int32, (TILE, PR), 0) + t * TILE
-            span = pl.ds(pl.multiple_of(t * TILE, TILE), TILE)
-            hot[i, span, 0:PR] = jnp.where(at == low, 1.0, 0.0).astype(BF16)
-            hot[i, span, PR:2 * PR] = jnp.where(at == high, 1.0, 0.0).astype(BF16)
+            at = lax.broadcasted_iota(jnp.int32, (PR, TILE), 1) + t * TILE
+            hot[i, t, 0:PR, :] = jnp.where(at == low, 1.0, 0.0).astype(BF16)
+            hot[i, t, PR:2 * PR, :] = jnp.where(at == high, 1.0, 0.0).astype(BF16)
             return 0
 
         lax.fori_loop(0, ROOT // TILE, make, 0)
@@ -88,6 +102,13 @@
             s2[s] = (s1[s].astype(F32) + r1[s].astype(F32)).astype(BF16)
             to = far if s < NODES // 2 else near
             second[s] = remote(s2.at[s], r2.at[s], s2_s.at[s], s2_r.at[s], (leaf, r, to))
+        if i == 0:
+            heard(0, 3)
+            tell(1, pair)
+        if i < 3:
+            heard(2 + i, 2)
+        if i < 2:
+            tell(3 + i, line_z)
     outs = []
     for i in range(NODES // 2):
         for h, s in enumerate((i, i + NODES // 2)):
@@ -101,22 +122,17 @@
             loads["p", s].wait()
             upd[:, h * PR:(h + 1) * PR] = dot_nt(solved, panel[s]).astype(BF16)
         if i < NODES // 2 - 1:
-
-            def add(t, _, i=i):
-                span = pl.ds(pl.multiple_of(t * TILE, TILE), TILE)
-                got = dot_nt(upd[...], hot[i, span, :])
+            for t in range(ROOT // TILE):
+                got = dot_nn(upd[...], hot[i, t])
                 acc[t] = got if i == 0 else acc[t] + got
-                return 0
-
-            lax.fori_loop(0, ROOT // TILE, add, 0)
         else:
+            heard(1, 1)
             pieces = {}
             for dc in (2, 1, 3, 0):
                 cb = (c + dc) % 4
                 for half in range(2):
                     t = cb * 2 + half
-                    span = pl.ds(pl.multiple_of(t * TILE, TILE), TILE)
-                    tile = (acc[t] + dot_nt(upd[...], hot[i, span, :])).astype(BF16)
+                    tile = (acc[t] + dot_nn(upd[...], hot[i, t])).astype(BF16)
                     for q in range(4):
                         cs[cb * 8 + half * 4 + q] = tile[:, q * 128:(q + 1) * 128]
                 for dr in (2, 1, 3, 0):
@@ -141,28 +157,35 @@
     for dz, copy in zip((4, 3, 5, 2, 6, 1, 7), zcopies):
         copy.wait_recv()
         total = total - zr[dz].astype(F32)
-    red[mine] = total.astype(BF16)
-    gathers = []
+    lanes = pl.ds(pl.multiple_of(k * 128, 128), 128)
+    red[r, :, lanes] = total.astype(BF16)
+    gathers = {}
     for dr in (2, 1, 3, 0):
         for dk in (1, 0):
             if dr == 0 and dk == 0:
                 continue
             j = dr * 2 + dk
-            gathers.append(remote(red.at[mine], red.at[mine], g_s.at[j], g_r.at[j], plane(dk, dr, 0)))
+            spot = red.at[r, :, lanes]
+            gathers[j] = remote(spot, spot, g_s.at[j], g_r.at[j], plane(dk, dr, 0))
     loads["droot"].wait()
-    for copy in gathers:
-        copy.wait_recv()
-    whole = dot_nt(red[0], droot[:, 0:128])
-    for q in range(1, 8):
-        whole = whole + dot_nt(red[q], droot[:, q * 128:(q + 1) * 128])
-    part[c] = whole
+    whole = jnp.zeros((B, 64), F32)
+    for dr in (0, 1, 3, 2):
+        for dk in (1, 0):
+            if dr or dk:
+                gathers[dr * 2 + dk].wait_recv()
+        rb = (r + 4 - dr) % 4
+        whole = whole + dot_nt(red[rb], droot[:, pl.ds(pl.multiple_of(rb * 256, 256), 256)])
+    half = B // 2
+    part[c] = jnp.concatenate([whole[0:half], whole[half:B]], axis=1)
     shares = []
     for dc in (2, 1, 3):
         shares.append(remote(part.at[c], part.at[c], p_s.at[dc], p_r.at[dc], (leaf, r, (c + dc) % 4)))
     for copy in shares:
         copy.wait_recv()
-    yroot_o[...] = (((part[0] + part[1]) + part[2]) + part[3]).astype(BF16)
-    for copies in (first.values(), second.values(), pieces.values(), zcopies, gathers, shares):
+    final = (((part[0] + part[1]) + part[2]) + part[3]).astype(BF16)
+    yroot_o[0:half, :] = final[:, 0:64]
+    yroot_o[half:B, :] = final[:, 64:128]
+    for copies in (first.values(), second.values(), pieces.values(), zcopies, gathers.values(), shares):
         for copy in copies:
             copy.wait_send()
     for out in outs:
@@ -189,17 +212,18 @@
             pltpu.VMEM((NODES, B, WC), BF16),
             pltpu.VMEM((NODES, B, WC), BF16),
             pltpu.VMEM((NODES, B, WC), BF16),
-            pltpu.VMEM((NODES // 2, ROOT, 2 * PR), BF16),
+            pltpu.VMEM((NODES // 2, ROOT // TILE, 2 * PR, TILE), BF16),
             pltpu.VMEM((B, 2 * PR), BF16),
             pltpu.VMEM((ROOT // TILE, B, TILE), F32),
             pltpu.VMEM((32, B, 128), BF16),
             pltpu.VMEM((32, B, 128), BF16),
             pltpu.VMEM((B, 128), BF16),
             pltpu.VMEM((8, B, 128), BF16),
-            pltpu.VMEM((8, B, 128), BF16),
-            pltpu.VMEM((4, B, 64), F32),
+            pltpu.VMEM((4, B, 256), BF16),
+            pltpu.VMEM((4, B // 2, 128), F32),
             dma((20,)), dma((8,)), dma((8,)), dma((8,)), dma((8,)), dma((8,)),
             dma((32,)), dma((32,)), dma((8,)), dma((8,)), dma((8,)), dma((8,)), dma((4,)), dma((4,)),
+            pltpu.SemaphoreType.REGULAR((5,)),
         ],
         compiler_params=pltpu.CompilerParams(
             collective_id=0, has_side_effects=True, vmem_limit_bytes=60 * 1024 * 1024),

time: 57.2 us -> 50.1 us (0.88)
  Pallas kernels: 52.5 us -> 45.6 us
    pallas_call x1, Pallas kernels: 52.5 us -> 45.6 us  [local(): pl.pallas_call(body, out_shape=(jax.ShapeDtypeStruct((1, NODES, B, WC), B...]
where the time goes in v2:
time: 50.1 us; the launch traced here: 49.4 us
  Pallas kernels  45.6 us (91%)
  local copies, waits for them, and re-layouts  3.19 us (6%)
  between operations  0.64 us (1%)
    pallas_call x1, Pallas kernels, local(): pl.pallas_call(body, out_shape=(jax.ShapeDtypeStruct((1, NODES, B, WC), B...  45.6 us
    unnamed x2, local copies, waits for them, and re-layouts  3.19 us

profile of v2, /device:TPU:32, one launch (start us, length us, event | category | flops | bytes accessed | tf_op | source)
XLA Modules:
  0.0 49.4 jit_solution(10058398586624484506)
XLA Ops:
  0.6 45.6 %substitute.1 = (bf16[1,8,64,512]{3,2,1,0:T(8,128)(2,1)}, bf16[64,64]{1,0:T(8,128)(2,1)}) custom-call(s32[1,8]{1,0:T(1,128)} %counts.1, bf16[1,8,64,512]{3,2,1,0:T(8,128)(2,1)} %rhs_h.1, bf16[1,8,512,512]{3,2,1,0:T(8,128)(2,1)} %dinv_h.1, bf16[1,8,256,512]{3,2,1,0:T(8,128)(2,1)} %panel_h.1, s32[1,8,1024]{2,1,0:T(8,128)} %rows_h.1, bf16[64,1024]{1,0:T(8,128)(2,1)} %rroot_h.1, ...), custom_call_target="tpu_custom_call" | custom-call | tf_op jit(solution)/shard_map/substitute/pallas_call | solution.py:198
  46.2 1.9 %copy.11 = bf16[1,8,64,512]{3,2,1,0:T(8,128)(2,1)} copy(bf16[1,8,64,512]{3,2,1,0:T(8,128)(2,1)} %get-tuple-element.4) | data formatting | bytes 1048576
  48.1 1.3 %copy.12 = bf16[64,64]{1,0:T(8,128)(2,1)} copy(bf16[64,64]{1,0:T(8,128)(2,1)} %get-tuple-element.5) | data formatting | bytes 16384

commit v3 on v2

--- a/solution.py
+++ b/solution.py
@@ -22,8 +22,8 @@
 
 def body(counts, rhs_h, dinv_h, panel_h, rows_h, rroot_h, droot_h, yleaf_h, yroot_o,
          rhs, dinv, panel, rows, rroot, droot, s1, r1, s2, r2, y, hot, upd, acc,
-         cs, cr, zs, zr, red, part, in_sem, s1_s, s1_r, s2_s, s2_r, y_sem,
-         c_s, c_r, z_s, z_r, g_s, g_r, p_s, p_r, relay):
+         cs, cr, zs, zr, red, root, in_sem, s1_s, s1_r, s2_s, s2_r, y_sem,
+         c_s, c_r, z_s, z_r, g_s, g_r, relay):
     leaf, r, c = lax.axis_index("leaf"), lax.axis_index("row"), lax.axis_index("col")
     z, k = leaf // 2, leaf % 2
     near = c + 1 - 2 * (c % 2)
@@ -36,20 +36,22 @@
 
     order = [s for i in range(NODES // 2) for s in (i, i + NODES // 2)]
     loads = {}
-    loads["rhs"] = load(rhs_h.at[0], rhs, 0)
     for s in order:
+        loads["r", s] = load(rhs_h.at[0, s], rhs.at[s], 20 + s)
         loads["d", s] = load(dinv_h.at[0, s], dinv.at[s], 1 + s)
     cut = pl.multiple_of(c * PR, PR)
     loads["rows"] = load(rows_h.at[0, :, pl.ds(cut, PR)], rows, 17)
     for s in order:
         loads["p", s] = load(panel_h.at[0, s], panel.at[s], 9 + s)
     loads["rroot"] = load(rroot_h, rroot, 18)
-    cut = pl.multiple_of(c * 1024, 1024)
-    loads["droot"] = load(droot_h.at[:, pl.ds(cut, 1024)], droot, 19)
+    loads["droot"] = load(droot_h, droot, 19)
 
     def plane(dk, dr, dc):
         return (z * 2 + (k + dk) % 2, (r + dr) % 4, (c + dc) % 4)
 
+    me = k * 16 + r * 4 + c
+    group = c * 2 + k
+    shifts = [(dk, dr, dc) for dc in (2, 1, 3, 0) for dr in (2, 1, 3, 0) for dk in (1, 0)]
     line_y = [plane(0, 0, dc) for dc in (1, 2, 3)]
     line_x = [plane(0, dr, 0) for dr in (1, 2, 3)]
     line_z = [(((z + dz) % 8) * 2 + k, r, c) for dz in (1, 7)]
@@ -65,16 +67,19 @@
     def heard(i, count):
         pl.semaphore_wait(relay.at[i], count)
 
+    def describe(src, dst, ss, rs, where):
+        return pltpu.make_async_remote_copy(
+            src_ref=src, dst_ref=dst, send_sem=ss, recv_sem=rs, device_id=where, device_id_type=MESH)
+
     def remote(src, dst, ss, rs, where):
-        copy = pltpu.make_async_remote_copy(
-            src_ref=src, dst_ref=dst, send_sem=ss, recv_sem=rs, device_id=where, device_id_type=MESH)
+        copy = describe(src, dst, ss, rs, where)
         copy.start()
         return copy
 
     lane = lax.broadcasted_iota(jnp.int32, (B, WC), 1)
     first, second = {}, {}
-    loads["rhs"].wait()
     for s in order:
+        loads["r", s].wait()
         loads["d", s].wait()
         masked = jnp.where(lane + c * WC < counts[0, s], rhs[s].astype(F32), 0.0).astype(BF16)
         s1[s] = dot_nt(masked, dinv[s]).astype(BF16)
@@ -127,75 +132,123 @@
                 acc[t] = got if i == 0 else acc[t] + got
         else:
             heard(1, 1)
-            pieces = {}
-            for dc in (2, 1, 3, 0):
-                cb = (c + dc) % 4
-                for half in range(2):
-                    t = cb * 2 + half
-                    tile = (acc[t] + dot_nn(upd[...], hot[i, t])).astype(BF16)
-                    for q in range(4):
-                        cs[cb * 8 + half * 4 + q] = tile[:, q * 128:(q + 1) * 128]
-                for dr in (2, 1, 3, 0):
-                    for dk in (1, 0):
-                        if dc == 0 and dr == 0 and dk == 0:
-                            continue
-                        kb, rb = (k + dk) % 2, (r + dr) % 4
-                        j = dc * 8 + dr * 2 + dk
-                        pieces[j] = remote(cs.at[cb * 8 + rb * 2 + kb], cr.at[j], c_s.at[j], c_r.at[j],
-                                           (z * 2 + kb, rb, cb))
-    mine = r * 2 + k
-    total = cs[c * 8 + mine].astype(F32)
-    for j in pieces:
-        pieces[j].wait_recv()
-        total = total + cr[j].astype(F32)
+            for t in range(8):
+                tile = (acc[t] + dot_nn(upd[...], hot[i, t])).astype(BF16)
+                for q in range(4):
+                    cs[t * 4 + q] = tile[:, q * 128:(q + 1) * 128]
+                for q in range(4):
+                    owner = (t % 2) * 16 + q * 4 + t // 2
+
+                    @pl.when(me == owner)
+                    def _(p=t * 4 + q, owner=owner):
+                        cr[owner] = cs[p]
+
+                    @pl.when(me != owner)
+                    def _(p=t * 4 + q, t=t, q=q):
+                        remote(cs.at[p], cr.at[me], c_s.at[p], c_r.at[me], (z * 2 + t % 2, q, t // 2))
+
+    total = jnp.zeros((B, 128), F32)
+    for slot in range(32):
+
+        @pl.when(me != slot)
+        def _(slot=slot):
+            describe(cs.at[0], cr.at[slot], c_s.at[0], c_r.at[slot], pair[0]).wait_recv()
+
+        total = total + cr[slot].astype(F32)
     zs[...] = total.astype(BF16)
-    zcopies = []
-    for dz in (4, 3, 5, 2, 6, 1, 7):
-        zcopies.append(remote(zs, zr.at[dz], z_s.at[dz], z_r.at[dz], (((z + dz) % 8) * 2 + k, r, c)))
+
+    def to_plane(to):
+        return describe(zs, zr.at[z], z_s.at[to], z_r.at[z], (to * 2 + k, r, c))
+
+    for to in range(8):
+
+        @pl.when((to >= group) & (to != z))
+        def _(to=to):
+            to_plane(to).start()
+
+    spot = red.at[group, :, pl.ds(pl.multiple_of(r * 128, 128), 128)]
+
+    def to_peer(shift):
+        j = shift[0] * 16 + shift[1] * 4 + shift[2]
+        return describe(spot, spot, g_s.at[j], g_r.at[group * 4 + r], plane(*shift))
+
     loads["rroot"].wait()
-    total = rroot[:, pl.ds(pl.multiple_of(mine * 128, 128), 128)].astype(F32) - zs[...].astype(F32)
-    for dz, copy in zip((4, 3, 5, 2, 6, 1, 7), zcopies):
-        copy.wait_recv()
-        total = total - zr[dz].astype(F32)
-    lanes = pl.ds(pl.multiple_of(k * 128, 128), 128)
-    red[r, :, lanes] = total.astype(BF16)
-    gathers = {}
-    for dr in (2, 1, 3, 0):
-        for dk in (1, 0):
-            if dr == 0 and dk == 0:
-                continue
-            j = dr * 2 + dk
-            spot = red.at[r, :, lanes]
-            gathers[j] = remote(spot, spot, g_s.at[j], g_r.at[j], plane(dk, dr, 0))
+
+    @pl.when(z >= group)
+    def _():
+        zr[z] = zs[...]
+        total = rroot[:, pl.ds(pl.multiple_of((k * 4 + r) * 128, 128), 128)].astype(F32)
+        for other in range(8):
+
+            @pl.when(z != other)
+            def _(other=other):
+                describe(zs, zr.at[other], z_s.at[other], z_r.at[other], pair[0]).wait_recv()
+
+        for other in range(8):
+            total = total - zr[other].astype(F32)
+        spot[...] = total.astype(BF16)
+        for shift in shifts[:-1]:
+            to_peer(shift).start()
+
     loads["droot"].wait()
-    whole = jnp.zeros((B, 64), F32)
-    for dr in (0, 1, 3, 2):
-        for dk in (1, 0):
-            if dr or dk:
-                gathers[dr * 2 + dk].wait_recv()
-        rb = (r + 4 - dr) % 4
-        whole = whole + dot_nt(red[rb], droot[:, pl.ds(pl.multiple_of(rb * 256, 256), 256)])
-    half = B // 2
-    part[c] = jnp.concatenate([whole[0:half], whole[half:B]], axis=1)
-    shares = []
-    for dc in (2, 1, 3):
-        shares.append(remote(part.at[c], part.at[c], p_s.at[dc], p_r.at[dc], (leaf, r, (c + dc) % 4)))
-    for copy in shares:
-        copy.wait_recv()
-    final = (((part[0] + part[1]) + part[2]) + part[3]).astype(BF16)
-    yroot_o[0:half, :] = final[:, 0:64]
-    yroot_o[half:B, :] = final[:, 64:128]
-    for copies in (first.values(), second.values(), pieces.values(), zcopies, gathers.values(), shares):
+    for g in range(8):
+
+        @pl.when(z >= g)
+        def _(g=g):
+            for q in range(4):
+
+                @pl.when((group != g) | (r != q))
+                def _(q=q):
+                    block = red.at[g, :, q * 128:(q + 1) * 128]
+                    describe(block, block, g_s.at[0], g_r.at[g * 4 + q], pair[0]).wait_recv()
+
+            share = dot_nt(red[g], droot[:, g * 512:(g + 1) * 512])
+            root[...] = share if g == 0 else root[...] + share
+
+    yroot_o[...] = root[...].astype(BF16)
+    for t in range(8):
+        for q in range(4):
+
+            @pl.when(me != (t % 2) * 16 + q * 4 + t // 2)
+            def _(p=t * 4 + q):
+                describe(cs.at[p], cr.at[me], c_s.at[p], c_r.at[me], pair[0]).wait_send()
+
+    for to in range(8):
+
+        @pl.when((to >= group) & (to != z))
+        def _(to=to):
+            to_plane(to).wait_send()
+
+    @pl.when(z >= group)
+    def _():
+        for shift in shifts[:-1]:
+            to_peer(shift).wait_send()
+
+    for copies in (first.values(), second.values()):
         for copy in copies:
             copy.wait_send()
     for out in outs:
         out.wait()
 
 
+def store(y, root, y_out, root_out, y_v, root_v, sem):
+    copies = [pltpu.make_async_copy(y.at[0, pl.ds(i * 2, 2)], y_v.at[pl.ds(i * 2, 2)], sem.at[i]) for i in range(4)]
+    copies.append(pltpu.make_async_copy(root, root_v, sem.at[4]))
+    outs = [pltpu.make_async_copy(y_v.at[pl.ds(i * 2, 2)], y_out.at[0, pl.ds(i * 2, 2)], sem.at[5 + i]) for i in range(4)]
+    outs.append(pltpu.make_async_copy(root_v, root_out, sem.at[9]))
+    for copy in copies:
+        copy.start()
+    for copy, out in zip(copies, outs):
+        copy.wait()
+        out.start()
+    for out in outs:
+        out.wait()
+
+
 def local(rhs_leaf, dinv_leaf, panel_leaf, counts, row_index, rhs_root, dinv_root):
     anywhere = pl.BlockSpec(memory_space=pl.ANY)
     dma = pltpu.SemaphoreType.DMA
-    return pl.pallas_call(
+    y_leaf, y_root = pl.pallas_call(
         body,
         out_shape=(jax.ShapeDtypeStruct((1, NODES, B, WC), BF16), jax.ShapeDtypeStruct((B, 64), BF16)),
         in_specs=[pl.BlockSpec(memory_space=pltpu.SMEM)] + [anywhere] * 6,
@@ -206,7 +259,7 @@
             pltpu.VMEM((NODES, PR, WC), BF16),
             pltpu.VMEM((NODES, PR), jnp.int32),
             pltpu.VMEM((B, 1024), BF16),
-            pltpu.VMEM((64, 1024), BF16),
+            pltpu.VMEM((64, ROOT), BF16),
             pltpu.VMEM((NODES, B, WC), BF16),
             pltpu.VMEM((NODES, B, WC), BF16),
             pltpu.VMEM((NODES, B, WC), BF16),
@@ -219,16 +272,25 @@
             pltpu.VMEM((32, B, 128), BF16),
             pltpu.VMEM((B, 128), BF16),
             pltpu.VMEM((8, B, 128), BF16),
-            pltpu.VMEM((4, B, 256), BF16),
-            pltpu.VMEM((4, B // 2, 128), F32),
-            dma((20,)), dma((8,)), dma((8,)), dma((8,)), dma((8,)), dma((8,)),
-            dma((32,)), dma((32,)), dma((8,)), dma((8,)), dma((8,)), dma((8,)), dma((4,)), dma((4,)),
+            pltpu.VMEM((8, B, 512), BF16),
+            pltpu.VMEM((B, 64), F32),
+            dma((28,)), dma((8,)), dma((8,)), dma((8,)), dma((8,)), dma((8,)),
+            dma((32,)), dma((32,)), dma((8,)), dma((8,)), dma((32,)), dma((32,)),
             pltpu.SemaphoreType.REGULAR((5,)),
         ],
         compiler_params=pltpu.CompilerParams(
             collective_id=0, has_side_effects=True, vmem_limit_bytes=60 * 1024 * 1024),
         name="substitute",
     )(counts, rhs_leaf, dinv_leaf, panel_leaf, row_index, rhs_root, dinv_root)
+    return pl.pallas_call(
+        store,
+        out_shape=(jax.ShapeDtypeStruct((1, NODES, B, WC), BF16), jax.ShapeDtypeStruct((B, 64), BF16)),
+        in_specs=[anywhere] * 2,
+        out_specs=(anywhere, anywhere),
+        scratch_shapes=[pltpu.VMEM((NODES, B, WC), BF16), pltpu.VMEM((B, 64), BF16), dma((10,))],
+        compiler_params=pltpu.CompilerParams(vmem_limit_bytes=60 * 1024 * 1024),
+        name="store",
+    )(y_leaf, y_root)
 
 
 def solution(mesh):

time: 50.1 us -> 47.4 us (0.946)
  local copies, waits for them, and re-layouts: 3.19 us -> 0 us
  Pallas kernels: 45.6 us -> 46.5 us
    unnamed x2 -> x0, local copies, waits for them, and re-layouts: 3.19 us -> none
    pallas_call x0 -> x1, Pallas kernels: none -> 1.84 us  [local(): pl.pallas_call(store, out_shape=(jax.ShapeDtypeStruct((1, NODES, B, WC),...]
    pallas_call x1, Pallas kernels: 45.6 us -> 44.6 us  [local(): pl.pallas_call(body, out_shape=(jax.ShapeDtypeStruct((1, NODES, B, WC), B...]
where the time goes in v3:
time: 47.4 us; the launch traced here: 47.1 us
  Pallas kernels  46.5 us (98%)
  between operations  0.64 us (1%)
    pallas_call x1, Pallas kernels, local(): pl.pallas_call(body, out_shape=(jax.ShapeDtypeStruct((1, NODES, B, WC), B...  44.6 us
    pallas_call x1, Pallas kernels, local(): pl.pallas_call(store, out_shape=(jax.ShapeDtypeStruct((1, NODES, B, WC),...  1.84 us

profile of v3, /device:TPU:32, one launch (start us, length us, event | category | flops | bytes accessed | tf_op | source)
XLA Modules:
  0.0 47.1 jit_solution(2812141012185985554)
XLA Ops:
  0.6 44.6 %substitute.1 = (bf16[1,8,64,512]{3,2,1,0:T(8,128)(2,1)}, bf16[64,64]{1,0:T(8,128)(2,1)}) custom-call(s32[1,8]{1,0:T(1,128)} %counts.1, bf16[1,8,64,512]{3,2,1,0:T(8,128)(2,1)} %rhs_h.1, bf16[1,8,512,512]{3,2,1,0:T(8,128)(2,1)} %dinv_h.1, bf16[1,8,256,512]{3,2,1,0:T(8,128)(2,1)} %panel_h.1, s32[1,8,1024]{2,1,0:T(8,128)} %rows_h.1, bf16[64,1024]{1,0:T(8,128)(2,1)} %rroot_h.1, ...), custom_call_target="tpu_custom_call" | custom-call | tf_op jit(solution)/shard_map/substitute/pallas_call | solution.py:251
  45.3 1.8 %store.1 = (bf16[1,8,64,512]{3,2,1,0:T(8,128)(2,1)}, bf16[64,64]{1,0:T(8,128)(2,1)}) custom-call(bf16[1,8,64,512]{3,2,1,0:T(8,128)(2,1)} %get-tuple-element.4.y, bf16[64,64]{1,0:T(8,128)(2,1)} %get-tuple-element.5.root), custom_call_target="tpu_custom_call" | custom-call | tf_op jit(solution)/shard_map/store/pallas_call | solution.py:285

commit v4 on v3

--- a/solution.py
+++ b/solution.py
@@ -20,10 +20,10 @@
     return lax.dot_general(a, b, (((1,), (1,)), ((), ())), preferred_element_type=F32)
 
 
-def body(counts, rhs_h, dinv_h, panel_h, rows_h, rroot_h, droot_h, yleaf_h, yroot_o,
-         rhs, dinv, panel, rows, rroot, droot, s1, r1, s2, r2, y, hot, upd, acc,
+def body(counts_h, rhs_h, dinv_h, panel_h, rows_h, rroot_h, droot_h, yleaf_h, yroot_o,
+         counts, rhs, dinv, panel, rows, rroot, droot, s1, r1, s2, r2, y, wanted, hot, upd, acc, give, take,
          cs, cr, zs, zr, red, root, in_sem, s1_s, s1_r, s2_s, s2_r, y_sem,
-         c_s, c_r, z_s, z_r, g_s, g_r, relay):
+         c_s, c_r, z_s, z_r, g_s, g_r, u_s, u_r, relay):
     leaf, r, c = lax.axis_index("leaf"), lax.axis_index("row"), lax.axis_index("col")
     z, k = leaf // 2, leaf % 2
     near = c + 1 - 2 * (c % 2)
@@ -36,20 +36,14 @@
 
     order = [s for i in range(NODES // 2) for s in (i, i + NODES // 2)]
     loads = {}
+    loads["counts"] = load(counts_h, counts, 0)
     for s in order:
         loads["r", s] = load(rhs_h.at[0, s], rhs.at[s], 20 + s)
         loads["d", s] = load(dinv_h.at[0, s], dinv.at[s], 1 + s)
-    cut = pl.multiple_of(c * PR, PR)
-    loads["rows"] = load(rows_h.at[0, :, pl.ds(cut, PR)], rows, 17)
-    for s in order:
-        loads["p", s] = load(panel_h.at[0, s], panel.at[s], 9 + s)
-    loads["rroot"] = load(rroot_h, rroot, 18)
-    loads["droot"] = load(droot_h, droot, 19)
-
     def plane(dk, dr, dc):
         return (z * 2 + (k + dk) % 2, (r + dr) % 4, (c + dc) % 4)
 
-    me = k * 16 + r * 4 + c
+    spot16 = r * 4 + c
     group = c * 2 + k
     shifts = [(dk, dr, dc) for dc in (2, 1, 3, 0) for dr in (2, 1, 3, 0) for dk in (1, 0)]
     line_y = [plane(0, 0, dc) for dc in (1, 2, 3)]
@@ -60,6 +54,13 @@
     for where in line_y + line_x + pair + line_z:
         pl.semaphore_signal(barrier, inc=1, device_id=where, device_id_type=MESH)
 
+    cut = pl.multiple_of(c * PR, PR)
+    loads["rows"] = load(rows_h.at[0, :, pl.ds(cut, PR)], rows, 17)
+    for s in order:
+        loads["p", s] = load(panel_h.at[0, s], panel.at[s], 9 + s)
+    loads["rroot"] = load(rroot_h, rroot, 18)
+    loads["droot"] = load(droot_h, droot, 19)
+
     def tell(i, peers):
         for where in peers:
             pl.semaphore_signal(relay.at[i], inc=1, device_id=where, device_id_type=MESH)
@@ -78,34 +79,45 @@
 
     lane = lax.broadcasted_iota(jnp.int32, (B, WC), 1)
     first, second = {}, {}
-    for s in order:
-        loads["r", s].wait()
-        loads["d", s].wait()
-        masked = jnp.where(lane + c * WC < counts[0, s], rhs[s].astype(F32), 0.0).astype(BF16)
-        s1[s] = dot_nt(masked, dinv[s]).astype(BF16)
-        to = near if s < NODES // 2 else far
-        if s == order[0]:
+    loads["counts"].wait()
+    for i in range(NODES // 2):
+        both = (i, i + NODES // 2)
+        for s in both:
+            loads["r", s].wait()
+            loads["d", s].wait()
+        for s in both:
+            masked = jnp.where(lane + c * WC < counts[0, s], rhs[s].astype(F32), 0.0).astype(BF16)
+            s1[s] = dot_nt(masked, dinv[s]).astype(BF16)
+        if i == 0:
             pl.semaphore_wait(barrier, 9)
+        for s, to in zip(both, (near, far)):
+            first[s] = remote(s1.at[s], r1.at[s], s1_s.at[s], s1_r.at[s], (leaf, r, to))
+        if i == 0:
             tell(0, line_x)
             tell(2, line_z)
-        first[s] = remote(s1.at[s], r1.at[s], s1_s.at[s], s1_r.at[s], (leaf, r, to))
     loads["rows"].wait()
     targets = jnp.transpose(rows[...])
+    lanes = lax.broadcasted_iota(jnp.int32, (PR, 128), 1)
     for i in range(NODES // 2):
-        low = targets[:, i:i + 1]
-        high = targets[:, i + NODES // 2:i + NODES // 2 + 1]
-
-        def make(t, _, i=i, low=low, high=high):
-            at = lax.broadcasted_iota(jnp.int32, (PR, TILE), 1) + t * TILE
-            hot[i, t, 0:PR, :] = jnp.where(at == low, 1.0, 0.0).astype(BF16)
-            hot[i, t, PR:2 * PR, :] = jnp.where(at == high, 1.0, 0.0).astype(BF16)
+        for h in range(2):
+            node = i + h * NODES // 2
+            wanted[h] = jnp.broadcast_to(targets[:, node:node + 1], (PR, 128)) - lanes
+
+        def make(t, _, i=i):
+            for h in range(2):
+                want = wanted[h]
+                for q in range(4):
+                    hot[i, t, h * PR:(h + 1) * PR, q * 128:(q + 1) * 128] = jnp.where(
+                        want == t * TILE + q * 128, 1.0, 0.0).astype(BF16)
             return 0
 
         lax.fori_loop(0, ROOT // TILE, make, 0)
-        for s in (i, i + NODES // 2):
+        both = (i, i + NODES // 2)
+        for s in both:
             first[s].wait_recv()
+        for s in both:
             s2[s] = (s1[s].astype(F32) + r1[s].astype(F32)).astype(BF16)
-            to = far if s < NODES // 2 else near
+        for s, to in zip(both, (far, near)):
             second[s] = remote(s2.at[s], r2.at[s], s2_s.at[s], s2_r.at[s], (leaf, r, to))
         if i == 0:
             heard(0, 3)
@@ -114,43 +126,60 @@
             heard(2 + i, 2)
         if i < 2:
             tell(3 + i, line_z)
+    for s in order:
+        loads["p", s].wait()
+    base = c // 2
     outs = []
     for i in range(NODES // 2):
-        for h, s in enumerate((i, i + NODES // 2)):
+        both = (i, i + NODES // 2)
+        for s in both:
             second[s].wait_recv()
+        for h, s in enumerate(both):
             total = s2[s].astype(F32) + r2[s].astype(F32)
             solved = jnp.where(lane + r * WC < counts[0, s], total, 0.0).astype(BF16)
             y[s] = solved
+            upd[:, h * PR:(h + 1) * PR] = dot_nt(solved, panel[s]).astype(BF16)
+        for s in both:
             out = pltpu.make_async_copy(y.at[s], yleaf_h.at[0, s], y_sem.at[s])
-            out.start()
+            if i < NODES // 2 - 1:
+                out.start()
             outs.append(out)
-            loads["p", s].wait()
-            upd[:, h * PR:(h + 1) * PR] = dot_nt(solved, panel[s]).astype(BF16)
         if i < NODES // 2 - 1:
-            for t in range(ROOT // TILE):
-                got = dot_nn(upd[...], hot[i, t])
-                acc[t] = got if i == 0 else acc[t] + got
+            if i == 0:
+                acc[7 - 7 * base] = jnp.zeros((B, TILE), F32)
+            for t in range(ROOT // TILE - 1):
+                got = dot_nn(upd[...], hot[i, t + base])
+                acc[t + base] = got if i == 0 else acc[t + base] + got
         else:
             heard(1, 1)
-            for t in range(8):
-                tile = (acc[t] + dot_nn(upd[...], hot[i, t])).astype(BF16)
+            swaps = []
+            for j in range(4):
+                t = 2 * j + 1 - k
+                give[j] = (acc[t] + dot_nn(upd[...], hot[i, t])).astype(BF16)
+                swaps.append(remote(give.at[j], take.at[j], u_s.at[j], u_r.at[j], pair[0]))
+            for j in range(4):
+                t = 2 * j + k
+                tile = acc[t] + dot_nn(upd[...], hot[i, t])
+                swaps[j].wait_recv()
+                tile = (tile + take[j].astype(F32)).astype(BF16)
                 for q in range(4):
-                    cs[t * 4 + q] = tile[:, q * 128:(q + 1) * 128]
+                    cs[j * 4 + q] = tile[:, q * 128:(q + 1) * 128]
                 for q in range(4):
-                    owner = (t % 2) * 16 + q * 4 + t // 2
-
-                    @pl.when(me == owner)
-                    def _(p=t * 4 + q, owner=owner):
-                        cr[owner] = cs[p]
-
-                    @pl.when(me != owner)
-                    def _(p=t * 4 + q, t=t, q=q):
-                        remote(cs.at[p], cr.at[me], c_s.at[p], c_r.at[me], (z * 2 + t % 2, q, t // 2))
-
+
+                    @pl.when(spot16 == q * 4 + j)
+                    def _(q=q, j=j):
+                        cr[q * 4 + j] = cs[j * 4 + q]
+
+                    @pl.when(spot16 != q * 4 + j)
+                    def _(q=q, j=j):
+                        remote(cs.at[j * 4 + q], cr.at[spot16], c_s.at[j * 4 + q], c_r.at[spot16], (leaf, q, j))
+
+    for out in outs[-2:]:
+        out.start()
     total = jnp.zeros((B, 128), F32)
-    for slot in range(32):
-
-        @pl.when(me != slot)
+    for slot in range(16):
+
+        @pl.when(spot16 != slot)
         def _(slot=slot):
             describe(cs.at[0], cr.at[slot], c_s.at[0], c_r.at[slot], pair[0]).wait_recv()
 
@@ -206,12 +235,12 @@
             root[...] = share if g == 0 else root[...] + share
 
     yroot_o[...] = root[...].astype(BF16)
-    for t in range(8):
+    for j in range(4):
         for q in range(4):
 
-            @pl.when(me != (t % 2) * 16 + q * 4 + t // 2)
-            def _(p=t * 4 + q):
-                describe(cs.at[p], cr.at[me], c_s.at[p], c_r.at[me], pair[0]).wait_send()
+            @pl.when(spot16 != q * 4 + j)
+            def _(p=j * 4 + q):
+                describe(cs.at[p], cr.at[spot16], c_s.at[p], c_r.at[spot16], pair[0]).wait_send()
 
     for to in range(8):
 
@@ -224,7 +253,7 @@
         for shift in shifts[:-1]:
             to_peer(shift).wait_send()
 
-    for copies in (first.values(), second.values()):
+    for copies in (first.values(), second.values(), swaps):
         for copy in copies:
             copy.wait_send()
     for out in outs:
@@ -232,10 +261,11 @@
 
 
 def store(y, root, y_out, root_out, y_v, root_v, sem):
-    copies = [pltpu.make_async_copy(y.at[0, pl.ds(i * 2, 2)], y_v.at[pl.ds(i * 2, 2)], sem.at[i]) for i in range(4)]
-    copies.append(pltpu.make_async_copy(root, root_v, sem.at[4]))
-    outs = [pltpu.make_async_copy(y_v.at[pl.ds(i * 2, 2)], y_out.at[0, pl.ds(i * 2, 2)], sem.at[5 + i]) for i in range(4)]
-    outs.append(pltpu.make_async_copy(root_v, root_out, sem.at[9]))
+    copies = [pltpu.make_async_copy(root, root_v, sem.at[0])]
+    outs = [pltpu.make_async_copy(root_v, root_out, sem.at[1])]
+    for i in range(NODES):
+        copies.append(pltpu.make_async_copy(y.at[0, i], y_v.at[i], sem.at[2 + i]))
+        outs.append(pltpu.make_async_copy(y_v.at[i], y_out.at[0, i], sem.at[10 + i]))
     for copy in copies:
         copy.start()
     for copy, out in zip(copies, outs):
@@ -251,9 +281,10 @@
     y_leaf, y_root = pl.pallas_call(
         body,
         out_shape=(jax.ShapeDtypeStruct((1, NODES, B, WC), BF16), jax.ShapeDtypeStruct((B, 64), BF16)),
-        in_specs=[pl.BlockSpec(memory_space=pltpu.SMEM)] + [anywhere] * 6,
+        in_specs=[anywhere] * 7,
         out_specs=(anywhere, pl.BlockSpec(memory_space=pltpu.VMEM)),
         scratch_shapes=[
+            pltpu.SMEM((1, NODES), jnp.int32),
             pltpu.VMEM((NODES, B, WC), BF16),
             pltpu.VMEM((NODES, WC, WC), BF16),
             pltpu.VMEM((NODES, PR, WC), BF16),
@@ -265,17 +296,20 @@
             pltpu.VMEM((NODES, B, WC), BF16),
             pltpu.VMEM((NODES, B, WC), BF16),
             pltpu.VMEM((NODES, B, WC), BF16),
+            pltpu.VMEM((2, PR, 128), jnp.int32),
             pltpu.VMEM((NODES // 2, ROOT // TILE, 2 * PR, TILE), BF16),
             pltpu.VMEM((B, 2 * PR), BF16),
             pltpu.VMEM((ROOT // TILE, B, TILE), F32),
-            pltpu.VMEM((32, B, 128), BF16),
-            pltpu.VMEM((32, B, 128), BF16),
+            pltpu.VMEM((4, B, TILE), BF16),
+            pltpu.VMEM((4, B, TILE), BF16),
+            pltpu.VMEM((16, B, 128), BF16),
+            pltpu.VMEM((16, B, 128), BF16),
             pltpu.VMEM((B, 128), BF16),
             pltpu.VMEM((8, B, 128), BF16),
             pltpu.VMEM((8, B, 512), BF16),
             pltpu.VMEM((B, 64), F32),
             dma((28,)), dma((8,)), dma((8,)), dma((8,)), dma((8,)), dma((8,)),
-            dma((32,)), dma((32,)), dma((8,)), dma((8,)), dma((32,)), dma((32,)),
+            dma((16,)), dma((16,)), dma((8,)), dma((8,)), dma((32,)), dma((32,)), dma((4,)), dma((4,)),
             pltpu.SemaphoreType.REGULAR((5,)),
         ],
         compiler_params=pltpu.CompilerParams(
@@ -287,7 +321,7 @@
         out_shape=(jax.ShapeDtypeStruct((1, NODES, B, WC), BF16), jax.ShapeDtypeStruct((B, 64), BF16)),
         in_specs=[anywhere] * 2,
         out_specs=(anywhere, anywhere),
-        scratch_shapes=[pltpu.VMEM((NODES, B, WC), BF16), pltpu.VMEM((B, 64), BF16), dma((10,))],
+        scratch_shapes=[pltpu.VMEM((NODES, B, WC), BF16), pltpu.VMEM((B, 64), BF16), dma((18,))],
         compiler_params=pltpu.CompilerParams(vmem_limit_bytes=60 * 1024 * 1024),
         name="store",
     )(y_leaf, y_root)

time: 47.4 us -> 46.4 us (0.979)
  Pallas kernels: 46.5 us -> 45.2 us
    pallas_call x1, Pallas kernels: 44.6 us -> 43.3 us  [local(): pl.pallas_call(body, out_shape=(jax.ShapeDtypeStruct((1, NODES, B, WC), B...]
where the time goes in v4:
time: 46.4 us; the launch traced here: 45.8 us
  Pallas kernels  45.2 us (97%)
  between operations  0.64 us (1%)
    pallas_call x1, Pallas kernels, local(): pl.pallas_call(body, out_shape=(jax.ShapeDtypeStruct((1, NODES, B, WC), B...  43.3 us
    pallas_call x1, Pallas kernels, local(): pl.pallas_call(store, out_shape=(jax.ShapeDtypeStruct((1, NODES, B, WC),...  1.86 us

profile of v4, /device:TPU:32, one launch (start us, length us, event | category | flops | bytes accessed | tf_op | source)
XLA Modules:
  0.0 45.8 jit_solution(14173861306345202837)
XLA Ops:
  0.6 43.3 %substitute.1 = (bf16[1,8,64,512]{3,2,1,0:T(8,128)(2,1)}, bf16[64,64]{1,0:T(8,128)(2,1)}) custom-call(s32[1,8]{1,0:T(1,128)} %counts_h.1, bf16[1,8,64,512]{3,2,1,0:T(8,128)(2,1)} %rhs_h.1, bf16[1,8,512,512]{3,2,1,0:T(8,128)(2,1)} %dinv_h.1, bf16[1,8,256,512]{3,2,1,0:T(8,128)(2,1)} %panel_h.1, s32[1,8,1024]{2,1,0:T(8,128)} %rows_h.1, ...), custom_call_target="tpu_custom_call" | custom-call | tf_op jit(solution)/shard_map/substitute/pallas_call | solution.py:281
  43.9 1.9 %store.1 = (bf16[1,8,64,512]{3,2,1,0:T(8,128)(2,1)}, bf16[64,64]{1,0:T(8,128)(2,1)}) custom-call(bf16[1,8,64,512]{3,2,1,0:T(8,128)(2,1)} %get-tuple-element.4.y, bf16[64,64]{1,0:T(8,128)(2,1)} %get-tuple-element.5.root), custom_call_target="tpu_custom_call" | custom-call | tf_op jit(solution)/shard_map/store/pallas_call | solution.py:319

commit v5 on v4

--- a/solution.py
+++ b/solution.py
@@ -45,7 +45,9 @@
 
     spot16 = r * 4 + c
     group = c * 2 + k
-    shifts = [(dk, dr, dc) for dc in (2, 1, 3, 0) for dr in (2, 1, 3, 0) for dk in (1, 0)]
+    early = [(1, dr, 0) for dr in (2, 1, 3, 0)]
+    others = [(dk, dr, dc) for dc in (2, 1, 3, 0) for dr in (2, 1, 3, 0) for dk in (1, 0)]
+    shifts = early + [shift for shift in others if shift not in early and any(shift)]
     line_y = [plane(0, 0, dc) for dc in (1, 2, 3)]
     line_x = [plane(0, dr, 0) for dr in (1, 2, 3)]
     line_z = [(((z + dz) % 8) * 2 + k, r, c) for dz in (1, 7)]
@@ -216,7 +218,7 @@
         for other in range(8):
             total = total - zr[other].astype(F32)
         spot[...] = total.astype(BF16)
-        for shift in shifts[:-1]:
+        for shift in shifts:
             to_peer(shift).start()
 
     loads["droot"].wait()
@@ -250,7 +252,7 @@
 
     @pl.when(z >= group)
     def _():
-        for shift in shifts[:-1]:
+        for shift in shifts:
             to_peer(shift).wait_send()
 
     for copies in (first.values(), second.values(), swaps):

time: 46.4 us -> 46.2 us (level)
  no operation moved by 1% of the time
where the time goes in v5:
time: 46.2 us; the launch traced here: 46 us
  Pallas kernels  45.3 us (98%)
  between operations  0.64 us (1%)
    pallas_call x1, Pallas kernels, local(): pl.pallas_call(body, out_shape=(jax.ShapeDtypeStruct((1, NODES, B, WC), B...  43.5 us
    pallas_call x1, Pallas kernels, local(): pl.pallas_call(store, out_shape=(jax.ShapeDtypeStruct((1, NODES, B, WC),...  1.86 us

profile of v5, /device:TPU:32, one launch (start us, length us, event | category | flops | bytes accessed | tf_op | source)
XLA Modules:
  0.0 46.0 jit_solution(7467875136123518195)
XLA Ops:
  0.6 43.5 %substitute.1 = (bf16[1,8,64,512]{3,2,1,0:T(8,128)(2,1)}, bf16[64,64]{1,0:T(8,128)(2,1)}) custom-call(s32[1,8]{1,0:T(1,128)} %counts_h.1, bf16[1,8,64,512]{3,2,1,0:T(8,128)(2,1)} %rhs_h.1, bf16[1,8,512,512]{3,2,1,0:T(8,128)(2,1)} %dinv_h.1, bf16[1,8,256,512]{3,2,1,0:T(8,128)(2,1)} %panel_h.1, s32[1,8,1024]{2,1,0:T(8,128)} %rows_h.1, ...), custom_call_target="tpu_custom_call" | custom-call | tf_op jit(solution)/shard_map/substitute/pallas_call | solution.py:283
  44.1 1.9 %store.1 = (bf16[1,8,64,512]{3,2,1,0:T(8,128)(2,1)}, bf16[64,64]{1,0:T(8,128)(2,1)}) custom-call(bf16[1,8,64,512]{3,2,1,0:T(8,128)(2,1)} %get-tuple-element.4.y, bf16[64,64]{1,0:T(8,128)(2,1)} %get-tuple-element.5.root), custom_call_target="tpu_custom_call" | custom-call | tf_op jit(solution)/shard_map/store/pallas_call | solution.py:321
